TPU v7x, 32 devices: a whole 2x2x4 slice. The times are simulated.
32 devices in a mesh: tm: 8 (over z, x), clip: 4 (over y, core).
Axes of the slice: x: 2, y: 2, z: 4, core: 2. Of those that a mesh axis runs over, the one named last changes fastest.
Arguments:
- video: float32 [4, 8, 16, 32, 320], P('clip', 'tm'), may hold values from -6 to 6
- spatial_w: bfloat16 [9, 320, 320], P(None, 'clip'), may hold values from -0.109375 to 0.109375
- spatial_b: float32 [320], replicated, may hold values from -3 to 3
- temporal_w: float32 [3, 320, 320], P(None, 'clip'), may hold values from -0.1875 to 0.1875
- cotangent: float32 [4, 8, 16, 32, 320], P('clip', 'tm'), may hold values from -6 to 6
Outputs:
- output: float32 [4, 8, 16, 32, 320], P('clip', 'tm')
- grad_video: float32 [4, 8, 16, 32, 320], P('clip', 'tm')
- grad_temporal: float32 [3, 320, 320], P(None, 'clip')
All inputs are finite; a program needn't handle non-finite values.
Results may differ from a plain program's by a relative error of at most 0.0049.
Values may be sent and summed in bfloat16 or wider, within the bound.
A program may use at most 64 MiB of HBM per device.

v0:
```python
import math
import jax
import jax.numpy as jnp
from jax import lax
from jax.sharding import PartitionSpec as P


def padded_2(cells, sides, width):
    for axis, dim in sides:
        count = lax.axis_size(axis)
        ends = count - 1
        head = lax.slice_in_dim(cells, 0, width, axis=dim)
        tail = lax.slice_in_dim(cells, cells.shape[dim] - width, cells.shape[dim], axis=dim)
        cells = jnp.concatenate(
            [
                lax.ppermute(tail, axis, [(i, (i + 1) % count) for i in range(ends)]),
                cells,
                lax.ppermute(head, axis, [((i + 1) % count, i) for i in range(ends)]),
            ],
            axis=dim,
        )
    return cells


def outer_dot(left, right):
    return lax.dot_general(
        left, right, (((0,), (0,)), ((), ())), preferred_element_type=jnp.float32
    )


def transpose_dot(left, right):
    return lax.dot_general(
        left, right, (((1,), (1,)), ((), ())), preferred_element_type=jnp.float32
    )


def on_device(video, spatial_w, spatial_b, temporal_w, cotangent):
    clips, frames, height, width, chans = video.shape
    row_count = clips * frames * height * width
    video_b = video.astype(jnp.bfloat16)
    padded = jnp.pad(video_b, ((0, 0), (0, 0), (1, 1), (1, 1), (0, 0)))
    temporal_b = temporal_w.astype(jnp.bfloat16)
    spatial_all, temporal_all = (
        lax.all_gather(spatial_w, "clip", axis=1, tiled=True),
        lax.all_gather(temporal_b, "clip", axis=1, tiled=True),
    )
    spatial = jnp.zeros((row_count, chans), jnp.float32)
    for shift_y in range(3):
        for shift_x in range(3):
            window = padded[:, :, shift_y : shift_y + height, shift_x : shift_x + width, :].reshape(
                row_count, chans
            )
            spatial = spatial + jnp.dot(
                window, spatial_all[3 * shift_y + shift_x], preferred_element_type=jnp.float32
            )
    spatial = spatial + spatial_b
    sigmoid_s = jax.nn.sigmoid(spatial)
    hidden = (spatial * sigmoid_s).astype(jnp.bfloat16).reshape(clips, frames, height, width, chans)
    hidden_pad = padded_2(hidden, (("tm", 1),), 1)
    temporal = jnp.zeros((row_count, chans), jnp.float32)
    for kernel_tap in range(3):
        shifted = hidden_pad[:, kernel_tap : kernel_tap + frames].reshape(row_count, chans)
        temporal = temporal + jnp.dot(
            shifted, temporal_all[kernel_tap], preferred_element_type=jnp.float32
        )
    output = video + temporal.reshape(video.shape)
    cot_b = cotangent.astype(jnp.bfloat16)
    cot_flat = cot_b.reshape(row_count, chans)
    cot_pad = padded_2(cot_b, (("tm", 1),), 1)
    grad_hidden = jnp.zeros((row_count, chans), jnp.float32)
    grads = []
    for kernel_tap in range(3):
        shifted_cot = cot_pad[:, 2 - kernel_tap : 2 - kernel_tap + frames].reshape(row_count, chans)
        grad_hidden = grad_hidden + transpose_dot(shifted_cot, temporal_all[kernel_tap])
        shifted_hid = hidden_pad[:, kernel_tap : kernel_tap + frames].reshape(row_count, chans)
        grads.append(outer_dot(shifted_hid, cot_flat))
    local_grad = jnp.stack(grads)
    total_rows = row_count * lax.axis_size("tm") * lax.axis_size("clip")
    summed = lax.psum(local_grad, "tm")
    owned = lax.psum_scatter(summed, "clip", scatter_dimension=1, tiled=True)
    grad_temporal = owned * (1.0 / math.sqrt(total_rows))
    grad_spatial = (grad_hidden * sigmoid_s * (1.0 + spatial * (1.0 - sigmoid_s))).astype(
        jnp.bfloat16
    )
    grad_frames = jnp.pad(
        grad_spatial.reshape(clips, frames, height, width, chans),
        ((0, 0), (0, 0), (1, 1), (1, 1), (0, 0)),
    )
    grad_acc = cotangent.reshape(row_count, chans)
    for shift_y in range(3):
        for shift_x in range(3):
            window = grad_frames[
                :, :, 2 - shift_y : 2 - shift_y + height, 2 - shift_x : 2 - shift_x + width, :
            ].reshape(row_count, chans)
            grad_acc = grad_acc + transpose_dot(window, spatial_all[3 * shift_y + shift_x])
    grad_video = grad_acc.reshape(video.shape)
    return (output, grad_video, grad_temporal)


def solution(mesh):
    return jax.shard_map(
        on_device,
        mesh=mesh,
        in_specs=(
            P("clip", "tm", None, None, None),
            P(None, "clip", None),
            P(),
            P(None, "clip", None),
            P("clip", "tm", None, None, None),
        ),
        out_specs=(
            P("clip", "tm", None, None, None),
            P("clip", "tm", None, None, None),
            P(None, "clip", None),
        ),
        check_vma=False,
    )
```

profile of v0, /device:TPU:0, one launch (start us, length us, event | category | flops | bytes accessed | tf_op | source)
XLA Modules:
  0.0 184.8 jit_solution(11059689400053077663)
XLA Ops:
  7.2 0.0 copy-start.4
  7.2 0.0 all-gather.2.cloned.1.call-start
  7.2 0.7 all-gather.2.cloned.1.call-update
  7.9 0.0 reduce-scatter.2.cloned.1.call-start
  8.0 1.2 convert_element_type.21
  9.2 4.9 %collective-permute-start.3 = (bf16[1,1,16,32,320]{4,3,2,1,0:T(8,128)(2,1)S(1)}, bf16[1,1,16,32,320]{4,3,2,1,0:T(8,128)(2,1)S(1)}, u32[]{:S(2)}, u32[]{:S(2)}) collective-permute-start(bf16[1,1,16,32,320]{4,3,2,1,0:T(8,128)(2,1)S(1)} %convert_element_type.21), channel_id=1, source_target_pairs={{0,4},{4,8},{8,12},{12,16},{16,20},{20,24},{24,28},{1,5},{5,9},{9,... | collective-permute-start | bytes 983048 | tf_op jit(solution)/shard_map/ppermute | solution.py:16
  14.1 1.3 collective-permute-start.2
  15.5 0.0 copy-start.3
  15.5 10.1 %all_gather.7 = bf16[3,320,320]{2,1,0:T(8,128)(2,1)S(1)} all-gather(bf16[3,80,320]{2,1,0:T(8,128)(2,1)S(1)} %convert_element_type.20), channel_id=1, replica_groups=mesh['tm'=8,'clip'=4] {'clip'}, dimensions={1}, use_global_device_ids=true | all-gather | bytes 768000 | tf_op jit(solution)/shard_map/all_gather | solution.py:45
  25.6 1.8 pad_slice_fusion.8
  27.4 1.1 copy.16
  28.5 1.2 fusion.19
  29.7 1.1 collective-permute-done.3
  30.8 1.2 fusion.21
  32.0 4.5 %all-gather.2.cloned.1.call-done = bf16[9,320,320]{2,1,0:T(8,128)(2,1)} async-done(((bf16[9,80,320]{2,1,0:T(8,128)(2,1)}), bf16[9,320,320]{2,1,0:T(8,128)(2,1)}) %all-gather.2.cloned.1.call-update) | async-done | bytes 1843216 | tf_op jit(solution)/shard_map/all_gather | solution.py:44
  36.5 1.6 fusion.14
  38.1 1.5 convolution_add_fusion.14
  39.6 1.4 convolution_add_fusion.13
  41.0 0.4 convolution_add_fusion.12
  41.4 0.4 convolution_add_fusion.11
  41.8 0.2 copy-done.17
  42.0 0.4 convolution_add_fusion.10
  42.4 0.0 copy-done.16
  42.4 0.4 convolution_add_fusion.9
  42.8 0.1 copy-done.15
  42.9 0.4 convolution_add_fusion.8
  43.3 0.2 copy-done.20
  43.4 1.4 multiply_convert_fusion
  44.8 1.9 %copy.13 = bf16[512,320]{1,0:T(8,128)(2,1)} copy(bf16[512,320]{0,1:T(8,128)(2,1)} %get-tuple-element.22) | data formatting | bytes 655360 | tf_op jit(solution)/shard_map/convert_element_type | solution.py:58
  46.7 1.3 collective-permute-start.1
  48.0 5.9 %collective-permute-start = (bf16[1,1,16,32,320]{4,3,2,1,0:T(8,128)(2,1)}, bf16[1,1,16,32,320]{4,3,2,1,0:T(8,128)(2,1)}, u32[]{:S(2)}, u32[]{:S(2)}) collective-permute-start(bf16[1,1,16,32,320]{4,3,2,1,0:T(8,128)(2,1)} %bitcast.146), channel_id=1, source_target_pairs={{0,4},{4,8},{8,12},{12,16},{16,20},{20,24},{24,28},{1,5},{5,9},{9,... | collective-permute-start | bytes 983048 | tf_op jit(solution)/shard_map/ppermute | solution.py:16
  53.9 2.8 %fusion.9 = bf16[512,320]{0,1:T(8,128)(2,1)} fusion(f32[512,320]{0,1:T(8,128)} %fusion.21, f32[512,320]{0,1:T(8,128)} %fusion.19, bf16[512,320]{1,0:T(8,128)(2,1)} %bitcast.26, f32[512,320]{0,1:T(8,128)} %get-tuple-element.23, bf16[3,320,320]{2,1,0:T(8,128)(2,1)S(1)} %all_gather.7), kind=kOutput, calls=%fused_computation.25 | convolution fusion | flops 106659840 | bytes 2867200 | tf_op jit(solution)/shard_map/dot_general | solution.py:32
  56.7 1.9 %copy.15 = bf16[512,320]{1,0:T(8,128)(2,1)} copy(bf16[512,320]{0,1:T(8,128)(2,1)} %fusion.9) | data formatting | bytes 655360 | tf_op jit(solution)/shard_map/convert_element_type | solution.py:82
  58.6 4.4 %pad_slice_fusion.4 = (bf16[1,1,16,32,320]{4,3,2,1,0:T(8,128)(2,1)}, bf16[1,1,16,32,320]{4,3,2,1,0:T(8,128)(2,1)}, bf16[1,1,16,32,320]{4,3,2,1,0:T(8,128)(2,1)},...) fusion(bf16[1,1,16,32,320]{4,3,2,1,0:T(8,128)(2,1)} %bitcast.132), kind=kLoop, calls=%fused_computation.35 | loop fusion | bytes 2949120 | tf_op jit(solution)/shard_map/slice | solution.py:92
  63.0 1.2 fusion.15
  64.3 0.3 convolution_bitcast_fusion.1
  64.6 1.4 convolution_bitcast_fusion
  66.0 3.7 %collective-permute-done = bf16[1,1,16,32,320]{4,3,2,1,0:T(8,128)(2,1)} collective-permute-done((bf16[1,1,16,32,320]{4,3,2,1,0:T(8,128)(2,1)}, bf16[1,1,16,32,320]{4,3,2,1,0:T(8,128)(2,1)}, u32[]{:S(2)}, u32[]{:S(2)}) %collective-permute-start) | collective-permute-done | bytes 327712 | tf_op jit(solution)/shard_map/ppermute | solution.py:16
  69.6 1.3 convolution_bitcast_fusion.2
  71.0 1.2 pad_maximum_fusion
  72.3 0.0 reduce-scatter.2.cloned.1.call-update
  72.3 0.0 all-reduce.4.cloned.1.call-start
  72.3 1.4 fusion.16
  73.8 1.4 fusion.17
  75.2 0.4 fusion.18
  75.6 0.4 convolution_add_fusion.4
  76.0 0.4 convolution_add_fusion.3
  76.4 0.2 copy-done.12
  76.6 0.4 convolution_add_fusion.2
  77.0 0.1 copy-done.11
  77.0 0.4 convolution_add_fusion.1
  77.4 0.1 copy-done.8
  77.5 0.1 copy-done.19
  77.6 1.2 fusion.3
  78.9 2.3 %copy.17 = f32[512,320]{1,0:T(8,128)} copy(f32[512,320]{0,1:T(8,128)} %fusion.3) | data formatting | bytes 1310720 | tf_op jit(solution)/shard_map/add | solution.py:95
  81.1 0.4 fusion.20
  81.5 20.0 %reduce-scatter.2.cloned.1.call-done = f32[3,80,320]{2,1,0:T(8,128)} async-done(((f32[3,320,320]{2,1,0:T(8,128)}), f32[3,80,320]{2,1,0:T(8,128)}) %reduce-scatter.2.cloned.1.call-update) | async-done | bytes 307216 | tf_op jit(solution)/shard_map/reduce_scatter | solution.py:80
  101.5 0.0 all-reduce.4.cloned.1.call-update
  101.6 1.4 fusion.22
  103.0 2.3 %fusion.7 = f32[512,320]{0,1:T(8,128)} fusion(f32[512,320]{0,1:T(8,128)S(1)} %fusion.22, f32[512,320]{0,1:T(8,128)S(1)} %fusion.20, bf16[512,320]{1,0:T(8,128)(2,1)} %bitcast.19, bf16[3,320,320]{2,1,0:T(8,128)(2,1)S(1)} %all_gather.7), kind=kOutput, calls=%fused_computation.15 | convolution fusion | flops 105185280 | bytes 2539520 | tf_op jit(solution)/shard_map/dot_general | solution.py:63
  105.2 1.3 copy.14
  106.6 1.0 add.101
  107.6 69.0 %all-reduce.4.cloned.1.call-done = f32[3,80,320]{2,1,0:T(8,128)} async-done(((f32[3,80,320]{2,1,0:T(8,128)}), f32[3,80,320]{2,1,0:T(8,128)}) %all-reduce.4.cloned.1.call-update) | async-done | bytes 307216 | tf_op jit(solution)/shard_map/psum | solution.py:79
  176.5 1.7 broadcast_multiply_fusion
  (40 shorter events, 0.2 us)
Async XLA Ops:
  7.2 8.2 %copy-start.4 = (f32[1,1,16,32,320]{4,3,2,1,0:T(8,128)S(1)}, f32[1,1,16,32,320]{4,3,2,1,0:T(8,128)}, u32[]{:S(2)}) copy-start(f32[1,1,16,32,320]{4,3,2,1,0:T(8,128)} %param.5) | copy-start | bytes 1966084
  7.2 8.2 %copy-start.21 = (f32[3,80,320]{2,1,0:T(8,128)S(1)}, f32[3,80,320]{2,1,0:T(8,128)}, u32[]{:S(2)}) copy-start(f32[3,80,320]{2,1,0:T(8,128)} %param.8) | copy-start | bytes 921604
  7.2 29.3 %all-gather.2.cloned.1.call-start = ((), (), s32[]{:S(2)}) async-start(), calls=%async_computation.1 | async-start | bytes 2764800 | tf_op jit(solution)/shard_map/all_gather | solution.py:44
  7.9 93.6 %reduce-scatter.2.cloned.1.call-start = ((), (), s32[]{:S(2)}) async-start(), calls=%async_computation.2 | async-start | bytes 1843200 | tf_op jit(solution)/shard_map/reduce_scatter | solution.py:80
  9.2 21.7 %collective-permute-start.3 = (bf16[1,1,16,32,320]{4,3,2,1,0:T(8,128)(2,1)S(1)}, bf16[1,1,16,32,320]{4,3,2,1,0:T(8,128)(2,1)S(1)}, u32[]{:S(2)}, u32[]{:S(2)}) collective-permute-start(bf16[1,1,16,32,320]{4,3,2,1,0:T(8,128)(2,1)S(1)} %convert_element_type.21), channel_id=1, source_target_pairs={{0,4},{4,8},{8,12},{12,16},{16,20},{20,24},{24,28},{1,5},{5,9},{9,... | collective-permute-start | bytes 983048 | tf_op jit(solution)/shard_map/ppermute | solution.py:16
  14.1 39.9 %collective-permute-start.2 = (bf16[1,1,16,32,320]{4,3,2,1,0:T(8,128)(2,1)S(1)}, bf16[1,1,16,32,320]{4,3,2,1,0:T(8,128)(2,1)}, u32[]{:S(2)}, u32[]{:S(2)}) collective-permute-start(bf16[1,1,16,32,320]{4,3,2,1,0:T(8,128)(2,1)S(1)} %convert_element_type.21), channel_id=1, source_target_pairs={{4,0},{8,4},{12,8},{16,12},{20,16},{24,20},{28,24},{5,1},{9,5},{13... | collective-permute-start | bytes 983048 | tf_op jit(solution)/shard_map/ppermute | solution.py:18
  15.4 11.9 %copy-start.1 = (bf16[1,1,16,32,320]{4,3,2,1,0:T(8,128)(2,1)}, bf16[1,1,16,32,320]{4,3,2,1,0:T(8,128)(2,1)S(1)}, u32[]{:S(2)}) copy-start(bf16[1,1,16,32,320]{4,3,2,1,0:T(8,128)(2,1)S(1)} %convert_element_type.18) | copy-start | bytes 983044
  15.5 11.9 %copy-start.3 = (f32[1,1,16,32,320]{4,3,2,1,0:T(8,128)S(1)}, f32[1,1,16,32,320]{4,3,2,1,0:T(8,128)}, u32[]{:S(2)}) copy-start(f32[1,1,16,32,320]{4,3,2,1,0:T(8,128)} %param.9) | copy-start | bytes 1966084
  36.5 3.1 %copy-start = (bf16[9,320,320]{2,1,0:T(8,128)(2,1)S(1)}, bf16[9,320,320]{2,1,0:T(8,128)(2,1)}, u32[]{:S(2)}) copy-start(bf16[9,320,320]{2,1,0:T(8,128)(2,1)} %all-gather.2.cloned.1.call-done) | copy-start | bytes 5529604
  38.1 3.0 %copy-start.18 = (bf16[1,1,16,32,320]{4,3,2,1,0:T(8,128)(2,1)S(1)}, bf16[1,1,16,32,320]{4,3,2,1,0:T(8,128)(2,1)}, u32[]{:S(2)}) copy-start(bf16[1,1,16,32,320]{4,3,2,1,0:T(8,128)(2,1)} %get-tuple-element.17) | copy-start | bytes 983044
  39.6 1.9 %copy-start.2 = (bf16[1,1,16,32,320]{4,3,2,1,0:T(8,128)(2,1)S(1)}, bf16[1,1,16,32,320]{4,3,2,1,0:T(8,128)(2,1)}, u32[]{:S(2)}) copy-start(bf16[1,1,16,32,320]{4,3,2,1,0:T(8,128)(2,1)} %copy-done.1) | copy-start | bytes 983044
  41.0 1.0 copy-start.17
  41.4 1.0 copy-start.16
  41.8 1.1 copy-start.15
  42.4 1.0 copy-start.20
  42.4 1.0 copy-start.22
  46.7 17.9 %collective-permute-start.1 = (bf16[1,1,16,32,320]{4,3,2,1,0:T(8,128)(2,1)}, bf16[1,1,16,32,320]{4,3,2,1,0:T(8,128)(2,1)}, u32[]{:S(2)}, u32[]{:S(2)}) collective-permute-start(bf16[1,1,16,32,320]{4,3,2,1,0:T(8,128)(2,1)} %bitcast.145), channel_id=1, source_target_pairs={{4,0},{8,4},{12,8},{16,12},{20,16},{24,20},{28,24},{5,1},{9,5},{13... | collective-permute-start | bytes 983048 | tf_op jit(solution)/shard_map/ppermute | solution.py:18
  48.0 21.6 %collective-permute-start = (bf16[1,1,16,32,320]{4,3,2,1,0:T(8,128)(2,1)}, bf16[1,1,16,32,320]{4,3,2,1,0:T(8,128)(2,1)}, u32[]{:S(2)}, u32[]{:S(2)}) collective-permute-start(bf16[1,1,16,32,320]{4,3,2,1,0:T(8,128)(2,1)} %bitcast.146), channel_id=1, source_target_pairs={{0,4},{4,8},{8,12},{12,16},{16,20},{20,24},{24,28},{1,5},{5,9},{9,... | collective-permute-start | bytes 983048 | tf_op jit(solution)/shard_map/ppermute | solution.py:16
  58.6 5.6 %copy-start.6 = (bf16[512,320]{0,1:T(8,128)(2,1)S(1)}, bf16[512,320]{0,1:T(8,128)(2,1)}, u32[]{:S(2)}) copy-start(bf16[512,320]{0,1:T(8,128)(2,1)} %get-tuple-element.22) | copy-start | bytes 983044
  72.2 3.0 %copy-start.10 = (bf16[1,1,16,32,320]{4,3,2,1,0:T(8,128)(2,1)S(1)}, bf16[1,1,16,32,320]{4,3,2,1,0:T(8,128)(2,1)}, u32[]{:S(2)}) copy-start(bf16[1,1,16,32,320]{4,3,2,1,0:T(8,128)(2,1)} %get-tuple-element.12) | copy-start | bytes 983044
  72.3 104.3 %all-reduce.4.cloned.1.call-start = ((), (), s32[]{:S(2)}) async-start(), calls=%async_computation.3 | async-start | bytes 737280 | tf_op jit(solution)/shard_map/psum | solution.py:79
  72.3 3.3 %copy-start.9 = (f32[512,320]{0,1:T(8,128)S(1)}, f32[512,320]{0,1:T(8,128)}, u32[]{:S(2)}) copy-start(f32[512,320]{0,1:T(8,128)} %copy.16) | copy-start | bytes 1966084
  72.3 3.3 %copy-start.14 = (bf16[1,1,16,32,320]{4,3,2,1,0:T(8,128)(2,1)S(1)}, bf16[1,1,16,32,320]{4,3,2,1,0:T(8,128)(2,1)}, u32[]{:S(2)}) copy-start(bf16[1,1,16,32,320]{4,3,2,1,0:T(8,128)(2,1)} %get-tuple-element.13) | copy-start | bytes 983044
  73.8 2.2 %copy-start.13 = (bf16[1,1,16,32,320]{4,3,2,1,0:T(8,128)(2,1)S(1)}, bf16[1,1,16,32,320]{4,3,2,1,0:T(8,128)(2,1)}, u32[]{:S(2)}) copy-start(bf16[1,1,16,32,320]{4,3,2,1,0:T(8,128)(2,1)} %get-tuple-element.7) | copy-start | bytes 983044
  75.6 1.0 copy-start.12
  76.0 1.0 copy-start.11
  76.4 1.1 copy-start.8
  76.4 1.2 copy-start.19
  77.6 3.5 %copy-start.7 = (bf16[512,320]{0,1:T(8,128)(2,1)S(1)}, bf16[512,320]{0,1:T(8,128)(2,1)}, u32[]{:S(2)}) copy-start(bf16[512,320]{0,1:T(8,128)(2,1)} %get-tuple-element.22) | copy-start | bytes 983044
  102.9 3.7 %copy-start.5 = (f32[1,1,16,32,320]{4,3,2,1,0:T(8,128)S(1)}, f32[1,1,16,32,320]{4,3,2,1,0:T(8,128)}, u32[]{:S(2)}) copy-start(f32[1,1,16,32,320]{4,3,2,1,0:T(8,128)} %param.5) | copy-start | bytes 1966084
Sparse Core Ops, SparseCore 0:
  9.6 26.8 all-gather.1
  72.4 29.1 reduce-scatter.1
  104.9 71.5 all-reduce.3
where the time goes:
time: 186 us; the launch traced here: 185 us
  waiting for transfers between devices  99 us (53%)
  matrix products  27.1 us (15%)
  local copies, waits for them, and re-layouts  15.7 us (8%)
  between operations  14.2 us (8%)
  starting transfers between devices  13.5 us (7%)
  blocking collectives  10.1 us (5%)
  other arithmetic  5.23 us (3%)
    psum x1, waiting for transfers between devices, on_device(): summed = lax.psum(local_grad, 'tm')  69 us
    reduce_scatter x1, waiting for transfers between devices, on_device(): owned = lax.psum_scatter(summed, 'clip', scatter_dimension=1, tiled=True)  20 us
    dot_general x12, matrix products, transpose_dot(): lax.dot_general(left, right, (((1,), (1,)), ((), ())), preferred_element_...  12.3 us
    ppermute x2, starting transfers between devices, padded_2(): lax.ppermute(tail, axis, [(i, (i + 1) % count) for i in range(ends)])  10.8 us
    all_gather x1, blocking collectives, on_device(): lax.all_gather(temporal_b, 'clip', axis=1, tiled=True)  10.1 us
    dot_general x9, matrix products, on_device(): jnp.dot(window, spatial_all[3 * shift_y + shift_x], preferred_element_typ...  7.74 us
    ppermute x2, waiting for transfers between devices, padded_2(): lax.ppermute(tail, axis, [(i, (i + 1) % count) for i in range(ends)])  4.81 us
    all_gather x1, waiting for transfers between devices, on_device(): lax.all_gather(spatial_w, 'clip', axis=1, tiled=True)  4.46 us
  transfers between devices with their start and end apart: 7, of which 5 were waited for; matrix products, arithmetic and copies ran while one was open for 23% of the time, Pallas kernels for 0%

commit v1 on v0

--- a/solution.py
+++ b/solution.py
@@ -76,7 +76,7 @@
         grads.append(outer_dot(shifted_hid, cot_flat))
     local_grad = jnp.stack(grads)
     total_rows = row_count * lax.axis_size("tm") * lax.axis_size("clip")
-    summed = lax.psum(local_grad, "tm")
+    summed = jnp.sum(lax.all_gather(local_grad, "tm"), axis=0)
     owned = lax.psum_scatter(summed, "clip", scatter_dimension=1, tiled=True)
     grad_temporal = owned * (1.0 / math.sqrt(total_rows))
     grad_spatial = (grad_hidden * sigmoid_s * (1.0 + spatial * (1.0 - sigmoid_s))).astype(

time: 186 us -> 278 us (1.49)
  waiting for transfers between devices: 99 us -> 192 us
  other arithmetic: 5.23 us -> 13.9 us
  matrix products: 27.1 us -> 21.9 us
    all_gather x0 -> x1, waiting for transfers between devices: none -> 131 us  [on_device(): summed = jnp.sum(lax.all_gather(local_grad, 'tm'), axis=0)]
    psum x1 -> x0, waiting for transfers between devices: 69 us -> none  [on_device(): summed = lax.psum(local_grad, 'tm')]
    all_gather x1, waiting for transfers between devices: 4.46 us -> 24.8 us  [on_device(): lax.all_gather(spatial_w, 'clip', axis=1, tiled=True)]
    ppermute x2, waiting for transfers between devices: 4.81 us -> 15.6 us  [padded_2(): lax.ppermute(tail, axis, [(i, (i + 1) % count) for i in range(ends)])]
    reduce_scatter x1, waiting for transfers between devices: 20 us -> 13.4 us  [on_device(): owned = lax.psum_scatter(summed, 'clip', scatter_dimension=1, tiled=True)]
    reduce_sum x0 -> x1, other arithmetic: none -> 6.42 us  [on_device(): summed = jnp.sum(lax.all_gather(local_grad, 'tm'), axis=0)]
    ppermute x2, waiting for transfers between devices: 0.01 us -> 5.96 us  [padded_2(): lax.ppermute(head, axis, [((i + 1) % count, i) for i in range(ends)])]
  transfers between devices with their start and end apart: 7 -> 7, of which waited for: 5 -> 6; matrix products, arithmetic and copies ran while one was open for 23% -> 12% of each run, Pallas kernels for 0% -> 0%
where the time goes in v1:
time: 278 us; the launch traced here: 277 us
  waiting for transfers between devices  192 us (69%)
  matrix products  21.9 us (8%)
  local copies, waits for them, and re-layouts  15.6 us (6%)
  between operations  14.1 us (5%)
  other arithmetic  13.9 us (5%)
  starting transfers between devices  12.3 us (4%)
  blocking collectives  7.78 us (3%)
    all_gather x1, waiting for transfers between devices, on_device(): summed = jnp.sum(lax.all_gather(local_grad, 'tm'), axis=0)  131 us
    all_gather x1, waiting for transfers between devices, on_device(): lax.all_gather(spatial_w, 'clip', axis=1, tiled=True)  24.8 us
    ppermute x2, waiting for transfers between devices, padded_2(): lax.ppermute(tail, axis, [(i, (i + 1) % count) for i in range(ends)])  15.6 us
    reduce_scatter x1, waiting for transfers between devices, on_device(): owned = lax.psum_scatter(summed, 'clip', scatter_dimension=1, tiled=True)  13.4 us
    dot_general x12, matrix products, transpose_dot(): lax.dot_general(left, right, (((1,), (1,)), ((), ())), preferred_element_...  12.4 us
    ppermute x2, starting transfers between devices, padded_2(): lax.ppermute(tail, axis, [(i, (i + 1) % count) for i in range(ends)])  9.6 us
    all_gather x1, blocking collectives, on_device(): lax.all_gather(temporal_b, 'clip', axis=1, tiled=True)  7.78 us
    dot_general x9, matrix products, on_device(): jnp.dot(window, spatial_all[3 * shift_y + shift_x], preferred_element_typ...  6.49 us
  transfers between devices with their start and end apart: 7, of which 6 were waited for; matrix products, arithmetic and copies ran while one was open for 12% of the time, Pallas kernels for 0%

profile of v1, /device:TPU:0, one launch (start us, length us, event | category | flops | bytes accessed | tf_op | source)
XLA Modules:
  0.0 277.1 jit_solution(17036696377614891153)
XLA Ops:
  7.2 0.0 all-gather.4.cloned.1.call-start
  7.2 0.7 all-gather.4.cloned.1.call-update
  7.9 0.0 all-gather.6.cloned.1.call-start
  7.9 1.2 convert_element_type.18
  9.1 1.6 pad_slice_fusion.8
  10.7 24.8 %all-gather.4.cloned.1.call-done = bf16[9,320,320]{2,1,0:T(8,128)(2,1)} async-done(((bf16[9,80,320]{2,1,0:T(8,128)(2,1)}), bf16[9,320,320]{2,1,0:T(8,128)(2,1)}) %all-gather.4.cloned.1.call-update) | async-done | bytes 1843216 | tf_op jit(solution)/shard_map/all_gather | solution.py:44
  35.5 1.5 fusion.14
  37.0 1.5 convolution_add_fusion.14
  38.5 0.4 convolution_add_fusion.13
  38.9 0.4 convolution_add_fusion.12
  39.3 0.4 convolution_add_fusion.11
  39.7 0.2 copy-done.11
  39.9 0.4 convolution_add_fusion.10
  40.3 0.4 convolution_add_fusion.9
  40.7 0.4 convolution_add_fusion.8
  41.1 0.2 copy-done.18
  41.3 1.3 multiply_convert_fusion
  42.6 0.9 copy.18
  43.5 1.3 collective-permute-start.1
  44.8 1.2 convert_element_type.21
  46.0 4.6 %collective-permute-start = (bf16[1,1,16,32,320]{4,3,2,1,0:T(8,128)(2,1)}, bf16[1,1,16,32,320]{4,3,2,1,0:T(8,128)(2,1)S(1)}, u32[]{:S(2)}, u32[]{:S(2)}) collective-permute-start(bf16[1,1,16,32,320]{4,3,2,1,0:T(8,128)(2,1)} %bitcast.18), channel_id=1, source_target_pairs={{0,4},{4,8},{8,12},{12,16},{16,20},{20,24},{24,28},{1,5},{5,9},{9,... | collective-permute-start | bytes 983048 | tf_op jit(solution)/shard_map/ppermute | solution.py:16
  50.5 0.3 convolution_bitcast_fusion.1
  50.9 6.0 %collective-permute-done.1 = bf16[1,1,16,32,320]{4,3,2,1,0:T(8,128)(2,1)S(1)} collective-permute-done((bf16[1,1,16,32,320]{4,3,2,1,0:T(8,128)(2,1)}, bf16[1,1,16,32,320]{4,3,2,1,0:T(8,128)(2,1)S(1)}, u32[]{:S(2)}, u32[]{:S(2)}) %collective-permute-start.1) | collective-permute-done | bytes 327712 | tf_op jit(solution)/shard_map/ppermute | solution.py:18
  56.8 0.4 convolution_bitcast_fusion
  57.2 8.0 %collective-permute-done = bf16[1,1,16,32,320]{4,3,2,1,0:T(8,128)(2,1)S(1)} collective-permute-done((bf16[1,1,16,32,320]{4,3,2,1,0:T(8,128)(2,1)}, bf16[1,1,16,32,320]{4,3,2,1,0:T(8,128)(2,1)S(1)}, u32[]{:S(2)}, u32[]{:S(2)}) %collective-permute-start) | collective-permute-done | bytes 327712 | tf_op jit(solution)/shard_map/ppermute | solution.py:16
  65.2 0.4 convolution_bitcast_fusion.2
  65.6 1.3 pad_maximum_fusion
  66.9 0.0 reduce-scatter.2.cloned.1.call-start
  67.0 5.0 %collective-permute-start.3 = (bf16[1,1,16,32,320]{4,3,2,1,0:T(8,128)(2,1)S(1)}, bf16[1,1,16,32,320]{4,3,2,1,0:T(8,128)(2,1)}, u32[]{:S(2)}, u32[]{:S(2)}) collective-permute-start(bf16[1,1,16,32,320]{4,3,2,1,0:T(8,128)(2,1)S(1)} %convert_element_type.21), channel_id=1, source_target_pairs={{0,4},{4,8},{8,12},{12,16},{16,20},{20,24},{24,28},{1,5},{5,9},{9,... | collective-permute-start | bytes 983048 | tf_op jit(solution)/shard_map/ppermute | solution.py:16
  72.0 1.3 collective-permute-start.2
  73.3 1.1 convert_element_type.20
  74.4 7.8 %all_gather.13 = bf16[3,320,320]{2,1,0:T(8,128)(2,1)S(1)} all-gather(bf16[3,80,320]{2,1,0:T(8,128)(2,1)S(1)} %convert_element_type.20), channel_id=1, replica_groups=mesh['tm'=8,'clip'=4] {'clip'}, dimensions={1}, use_global_device_ids=true | all-gather | bytes 768000 | tf_op jit(solution)/shard_map/all_gather | solution.py:45
  82.1 1.2 fusion.19
  83.3 2.3 copy.21
  85.6 7.6 %collective-permute-done.3 = bf16[1,1,16,32,320]{4,3,2,1,0:T(8,128)(2,1)} collective-permute-done((bf16[1,1,16,32,320]{4,3,2,1,0:T(8,128)(2,1)S(1)}, bf16[1,1,16,32,320]{4,3,2,1,0:T(8,128)(2,1)}, u32[]{:S(2)}, u32[]{:S(2)}) %collective-permute-start.3) | collective-permute-done | bytes 327712 | tf_op jit(solution)/shard_map/ppermute | solution.py:16
  93.2 1.4 fusion.21
  94.6 1.9 fusion.9
  96.5 0.9 copy.20
  97.4 4.5 %pad_slice_fusion.4 = (bf16[1,1,16,32,320]{4,3,2,1,0:T(8,128)(2,1)}, bf16[1,1,16,32,320]{4,3,2,1,0:T(8,128)(2,1)}, bf16[1,1,16,32,320]{4,3,2,1,0:T(8,128)(2,1)},...) fusion(bf16[1,1,16,32,320]{4,3,2,1,0:T(8,128)(2,1)} %bitcast.134), kind=kLoop, calls=%fused_computation.35 | loop fusion | bytes 2949120 | tf_op jit(solution)/shard_map/slice | solution.py:92
  101.9 1.2 fusion.18
  103.1 1.2 fusion.17
  104.3 1.2 fusion.16
  105.6 131.1 %all-gather.6.cloned.1.call-done = f32[24,320,320]{2,1,0:T(8,128)} async-done(((f32[3,320,320]{2,1,0:T(8,128)}), f32[24,320,320]{2,1,0:T(8,128)}) %all-gather.6.cloned.1.call-update) | async-done | bytes 9830416 | tf_op jit(solution)/shard_map/all_gather | solution.py:79
  236.6 6.4 %reduce_sum.9 = f32[3,320,320]{2,1,0:T(8,128)} reduce(f32[8,3,320,320]{3,2,1,0:T(8,128)} %bitcast.123, f32[]{:T(128)} %constant.3.clone.1), dimensions={0}, to_apply=%region_0.1 | reduce | flops 2150400 | bytes 11059204 | tf_op jit(solution)/shard_map/reduce_sum | solution.py:79
  243.1 0.4 fusion.15
  243.5 1.6 convolution_add_fusion.4
  245.1 0.4 convolution_add_fusion.3
  245.5 0.4 convolution_add_fusion.2
  245.9 0.2 copy-done.7
  246.1 0.4 convolution_add_fusion.1
  246.5 0.1 copy-done.4
  246.6 0.2 copy-done.5
  246.8 0.4 copy-done.6
  247.2 0.1 copy-done.15
  247.3 1.2 fusion.3
  248.5 2.4 copy.22
  250.9 0.4 fusion.20
  251.3 0.4 fusion.22
  251.7 0.2 copy-done.17
  251.9 1.2 fusion.7
  253.1 1.3 copy.19
  254.5 1.0 add.99
  255.4 13.4 %reduce-scatter.2.cloned.1.call-done = f32[3,80,320]{2,1,0:T(8,128)} async-done(((f32[3,320,320]{2,1,0:T(8,128)}), f32[3,80,320]{2,1,0:T(8,128)}) %reduce-scatter.2.cloned.1.call-update) | async-done | bytes 307216 | tf_op jit(solution)/shard_map/reduce_scatter | solution.py:80
  268.8 1.7 broadcast_multiply_fusion
  (39 shorter events, 0.1 us)
Async XLA Ops:
  7.2 28.3 %all-gather.4.cloned.1.call-start = ((), (), s32[]{:S(2)}) async-start(), calls=%async_computation.1 | async-start | bytes 2764800 | tf_op jit(solution)/shard_map/all_gather | solution.py:44
  7.9 228.7 %all-gather.6.cloned.1.call-start = ((), (), s32[]{:S(2)}) async-start(), calls=%async_computation.3 | async-start | bytes 13271040 | tf_op jit(solution)/shard_map/all_gather | solution.py:79
  35.5 3.0 %copy-start = (bf16[9,320,320]{2,1,0:T(8,128)(2,1)S(1)}, bf16[9,320,320]{2,1,0:T(8,128)(2,1)}, u32[]{:S(2)}) copy-start(bf16[9,320,320]{2,1,0:T(8,128)(2,1)} %all-gather.4.cloned.1.call-done) | copy-start | bytes 5529604
  35.5 3.0 %copy-start.13 = (bf16[1,1,16,32,320]{4,3,2,1,0:T(8,128)(2,1)S(1)}, bf16[1,1,16,32,320]{4,3,2,1,0:T(8,128)(2,1)}, u32[]{:S(2)}) copy-start(bf16[1,1,16,32,320]{4,3,2,1,0:T(8,128)(2,1)} %get-tuple-element.16) | copy-start | bytes 983044
  37.0 1.9 copy-start.12
  38.9 1.0 copy-start.11
  39.3 1.0 copy-start.10
  40.3 1.0 copy-start.18
  40.3 1.0 copy-start.21
  42.6 14.6 %copy-start.2 = (bf16[512,320]{0,1:T(8,128)(2,1)}, bf16[512,320]{0,1:T(8,128)(2,1)S(1)}, u32[]{:S(2)}) copy-start(bf16[512,320]{0,1:T(8,128)(2,1)S(1)} %get-tuple-element.22) | copy-start | bytes 983044
  43.5 13.3 %collective-permute-start.1 = (bf16[1,1,16,32,320]{4,3,2,1,0:T(8,128)(2,1)}, bf16[1,1,16,32,320]{4,3,2,1,0:T(8,128)(2,1)S(1)}, u32[]{:S(2)}, u32[]{:S(2)}) collective-permute-start(bf16[1,1,16,32,320]{4,3,2,1,0:T(8,128)(2,1)} %bitcast.18), channel_id=1, source_target_pairs={{4,0},{8,4},{12,8},{16,12},{20,16},{24,20},{28,24},{5,1},{9,5},{13... | collective-permute-start | bytes 983048 | tf_op jit(solution)/shard_map/ppermute | solution.py:18
  46.0 19.3 %collective-permute-start = (bf16[1,1,16,32,320]{4,3,2,1,0:T(8,128)(2,1)}, bf16[1,1,16,32,320]{4,3,2,1,0:T(8,128)(2,1)S(1)}, u32[]{:S(2)}, u32[]{:S(2)}) collective-permute-start(bf16[1,1,16,32,320]{4,3,2,1,0:T(8,128)(2,1)} %bitcast.18), channel_id=1, source_target_pairs={{0,4},{4,8},{8,12},{12,16},{16,20},{20,24},{24,28},{1,5},{5,9},{9,... | collective-permute-start | bytes 983048 | tf_op jit(solution)/shard_map/ppermute | solution.py:16
  56.8 8.4 %copy-start.19 = (bf16[1,1,16,32,320]{4,3,2,1,0:T(8,128)(2,1)}, bf16[1,1,16,32,320]{4,3,2,1,0:T(8,128)(2,1)S(1)}, u32[]{:S(2)}) copy-start(bf16[1,1,16,32,320]{4,3,2,1,0:T(8,128)(2,1)S(1)} %collective-permute-done.1) | copy-start | bytes 983044
  65.2 1.7 copy-start.16
  66.9 201.9 %reduce-scatter.2.cloned.1.call-start = ((), (), s32[]{:S(2)}) async-start(), calls=%async_computation.2 | async-start | bytes 1843200 | tf_op jit(solution)/shard_map/reduce_scatter | solution.py:80
  67.0 26.2 %collective-permute-start.3 = (bf16[1,1,16,32,320]{4,3,2,1,0:T(8,128)(2,1)S(1)}, bf16[1,1,16,32,320]{4,3,2,1,0:T(8,128)(2,1)}, u32[]{:S(2)}, u32[]{:S(2)}) collective-permute-start(bf16[1,1,16,32,320]{4,3,2,1,0:T(8,128)(2,1)S(1)} %convert_element_type.21), channel_id=1, source_target_pairs={{0,4},{4,8},{8,12},{12,16},{16,20},{20,24},{24,28},{1,5},{5,9},{9,... | collective-permute-start | bytes 983048 | tf_op jit(solution)/shard_map/ppermute | solution.py:16
  72.0 22.6 %collective-permute-start.2 = (bf16[1,1,16,32,320]{4,3,2,1,0:T(8,128)(2,1)S(1)}, bf16[1,1,16,32,320]{4,3,2,1,0:T(8,128)(2,1)}, u32[]{:S(2)}, u32[]{:S(2)}) collective-permute-start(bf16[1,1,16,32,320]{4,3,2,1,0:T(8,128)(2,1)S(1)} %convert_element_type.21), channel_id=1, source_target_pairs={{4,0},{8,4},{12,8},{16,12},{20,16},{24,20},{28,24},{5,1},{9,5},{13... | collective-permute-start | bytes 983048 | tf_op jit(solution)/shard_map/ppermute | solution.py:18
  96.5 0.9 copy-start.14
  243.1 2.0 copy-start.9
  243.5 2.1 copy-start.8
  245.1 1.0 copy-start.7
  245.5 1.1 copy-start.4
  245.5 1.3 copy-start.5
  245.5 1.7 copy-start.6
  245.5 1.8 copy-start.15
  247.3 3.6 %copy-start.3 = (bf16[512,320]{0,1:T(8,128)(2,1)S(1)}, bf16[512,320]{0,1:T(8,128)(2,1)}, u32[]{:S(2)}) copy-start(bf16[512,320]{0,1:T(8,128)(2,1)} %copy-done.2) | copy-start | bytes 983044
  248.5 2.8 copy-start.20
  250.9 1.0 copy-start.17
  251.7 2.8 %copy-start.1 = (f32[1,1,16,32,320]{4,3,2,1,0:T(8,128)S(1)}, f32[1,1,16,32,320]{4,3,2,1,0:T(8,128)}, u32[]{:S(2)}) copy-start(f32[1,1,16,32,320]{4,3,2,1,0:T(8,128)} %param.5) | copy-start | bytes 1966084
Sparse Core Ops, SparseCore 0:
  9.5 25.9 all-gather.3
  67.1 169.5 all-gather.5
  243.2 25.6 reduce-scatter.1
